TPU v7x, 32 devices: a whole 2x2x4 slice. The times are simulated.
32 devices in a mesh: gx: 4 (over z), gy: 8 (over y, x, core).
Axes of the slice: x: 2, y: 2, z: 4, core: 2. Of those that a mesh axis runs over, the one named last changes fastest.
Arguments:
- centres: bfloat16 [131072, 256], P(('gx', 'gy')), may hold values from -20 to 20
- weights: float32 [16, 131072], P(None, ('gx', 'gy')), may hold values from -1 to 1
- targets: float32 [16, 256], P(None, ('gx', 'gy')), may hold values from -6 to 6
- batch_index: int32 [256], P(('gx', 'gy')), may hold values from 0 to 131071, as said below
- nystrom_index: int32 [2048], P(('gx', 'gy')), may hold values from 0 to 131071, as said below
- eigvecs: float32 [2048, 128], P(('gx', 'gy')), may hold values from -0.125 to 0.125
- scales: float32 [128], replicated, may hold values from 0.2 to 2
Outputs:
- residual: float32 [16, 256], P(None, ('gx', 'gy'))
- block_correction: float32 [16, 2048], P(None, ('gx', 'gy'))
Inputs may be any that keep to these rules, and one draw needn't show every extreme that they name: `batch_index`: the entries at positions j * 8 to (j + 1) * 8 - 1 name centres j * 4096 to (j + 1) * 4096 - 1, all different. `nystrom_index`: the entries at positions j * 64 to (j + 1) * 64 - 1 name centres j * 4096 to (j + 1) * 4096 - 1, all different.
All inputs are finite; a program needn't handle non-finite values.
Results may differ from a plain program's by a relative error of at most 0.0003.
Values may be sent and summed in bfloat16 or wider, within the bound.
A program may use at most 192 MiB of HBM per device.

v0:
```python
import jax
import jax.numpy as jnp
from jax import lax
from jax.sharding import PartitionSpec as P


def kernel_tile(points, point_norm, others, other_norm):
    width = float(points.shape[1]) ** 0.5
    inner = jnp.dot(points, others.T, preferred_element_type=jnp.float32)
    squared = point_norm[:, None] + other_norm[None, :] - 2.0 * inner
    return jnp.exp(-jnp.sqrt(jnp.maximum(squared, 1.0)) / width)


def combine_projection(partial_projection):
    return lax.psum(partial_projection, ("gx", "gy"))


def on_device(centres, weights, targets, batch_index, nystrom_index, eigvecs, scales):
    device_rank = lax.axis_index(("gx", "gy"))
    local_count = centres.shape[0]
    outputs = weights.shape[0]
    local_batch = batch_index - device_rank * local_count
    local_block = nystrom_index - device_rank * local_count
    batch_local = jnp.take(centres, local_batch, axis=0)
    centre_norm = jnp.sum(centres.astype(jnp.float32) ** 2, axis=1)
    rows_in = lax.all_gather(batch_local, ("gx", "gy"), axis=0, tiled=True)
    rows_norm = jnp.sum(rows_in.astype(jnp.float32) ** 2, axis=1)
    tile = kernel_tile(rows_in, rows_norm, centres, centre_norm)
    predicted = lax.dot_general(
        weights, tile, (((1,), (1,)), ((), ())), precision=lax.Precision.HIGHEST
    )
    block_tile = jnp.take(tile, local_block, axis=1)
    carried = block_tile.T
    gathered = jnp.concatenate([predicted, carried], axis=0)
    partial_prediction = gathered[:outputs]
    carried = gathered[outputs:]
    inner_sum = lax.psum(partial_prediction, "gy")
    reduced = lax.psum(inner_sum, "gx")
    targets_full = lax.all_gather(targets, ("gx", "gy"), axis=1, tiled=True)
    residual_full = reduced - targets_full
    residual_local = lax.dynamic_slice_in_dim(
        residual_full, device_rank * batch_local.shape[0], batch_local.shape[0], 1
    )
    along = jnp.dot(carried, residual_full.T, precision=lax.Precision.HIGHEST)
    projection = combine_projection(jnp.dot(eigvecs.T, along, precision=lax.Precision.HIGHEST))
    correction = jnp.dot(eigvecs * scales[None, :], projection, precision=lax.Precision.HIGHEST)
    return (residual_local, correction.T)


def solution(mesh):
    return jax.shard_map(
        on_device,
        mesh=mesh,
        in_specs=(
            P(("gx", "gy"), None),
            P(None, ("gx", "gy")),
            P(None, ("gx", "gy")),
            P(("gx", "gy")),
            P(("gx", "gy")),
            P(("gx", "gy"), None),
            P(),
        ),
        out_specs=(P(None, ("gx", "gy")), P(None, ("gx", "gy"))),
        check_vma=False,
    )
```

profile of v0, /device:TPU:14, one launch (start us, length us, event | category | flops | bytes accessed | tf_op | source)
XLA Modules:
  0.0 182.1 jit_solution(13803542961892802203)
XLA Ops:
  0.6 0.0 copy-start
  0.7 0.7 compare_and_fusion.1
  1.4 2.4 %gather_fusion = bf16[8,256]{1,0:T(8,128)(2,1)S(1)} fusion(bf16[4096,256]{1,0:T(8,128)(2,1)} %param.7, s32[1024]{0:T(1024)S(1)} %pad_clamp_fusion.1), kind=kCustom, calls=%fused_computation | custom fusion | bytes 8224 | tf_op jit(solution)/shard_map/jit(_take)/gather | solution.py:24
  3.8 0.1 broadcast_select_fusion
  3.9 29.1 %all_gather.6 = bf16[256,256]{1,0:T(8,128)(2,1)S(1)} all-gather(bf16[8,256]{1,0:T(8,128)(2,1)S(1)} %broadcast_select_fusion), channel_id=1, replica_groups=mesh['gx'=4,'gy'=8] {'gx','gy'}, dimensions={0}, use_global_device_ids=true | all-gather | bytes 135168 | tf_op jit(solution)/shard_map/all_gather | solution.py:26
  33.0 2.2 %multiply_reduce_fusion = f32[4096]{0:T(1024)S(1)} fusion(bf16[4096,256]{1,0:T(8,128)(2,1)} %param.7), kind=kLoop, calls=%fused_computation.9 | loop fusion | flops 3141632 | bytes 2113536 | tf_op jit(solution)/shard_map/reduce_sum | solution.py:25
  35.2 0.1 multiply_reduce_fusion.1
  35.3 3.8 %fusion.5 = f32[256,4096]{1,0:T(8,128)S(1)} fusion(bf16[256,256]{1,0:T(8,128)(2,1)S(1)} %all_gather.6, bf16[4096,256]{1,0:T(8,128)(2,1)} %param.7, f32[4096]{0:T(1024)S(1)} %multiply_reduce_fusion, f32[256]{0:T(256)S(1)} %multiply_reduce_fusion.1), kind=kOutput, calls=%fused_computation.8 | convolution fusion | flops 543162368 | bytes 6439936 | tf_op jit(solution)/shard_map/dot_general | solution.py:9
  39.2 0.0 copy-start.1
  39.2 1.9 %copy-done.1 = f32[256,4096]{1,0:T(8,128)} copy-done((f32[256,4096]{1,0:T(8,128)}, f32[256,4096]{1,0:T(8,128)S(1)}, u32[]{:S(2)}) %copy-start.1) | copy-done | bytes 4194328
  41.1 0.0 copy-done
  41.1 0.0 copy-start.3
  41.1 3.3 %convolution_bitcast_fusion = f32[16,256]{1,0:T(8,128)S(1)} fusion(f32[256,4096]{1,0:T(8,128)S(1)} %fusion.5, f32[16,4096]{1,0:T(8,128)S(1)} %copy-done), kind=kOutput, calls=%fused_computation.10 | convolution fusion | flops 201326592 | bytes 4472832 | tf_op jit(solution)/shard_map/dot_general | solution.py:29
  44.4 25.5 %psum.21 = f32[16,256]{1,0:T(8,128)S(1)} all-reduce(f32[16,256]{1,0:T(8,128)S(1)} %convolution_bitcast_fusion), channel_id=1, replica_groups=mesh['gx'=4,'gy'=8] {'gy'}, use_global_device_ids=true, to_apply=%region_2.3 | all-reduce | flops 4096 | bytes 32768 | tf_op jit(solution)/shard_map/psum | solution.py:37
  70.0 20.5 %psum.22 = f32[16,256]{1,0:T(8,128)S(1)} all-reduce(f32[16,256]{1,0:T(8,128)S(1)} %psum.21), channel_id=1, replica_groups=mesh['gx'=4,'gy'=8] {'gx'}, use_global_device_ids=true, to_apply=%region_3.4 | all-reduce | flops 4096 | bytes 32768 | tf_op jit(solution)/shard_map/psum | solution.py:38
  90.5 0.0 copy-done.3
  90.5 32.1 %all_gather.7 = f32[16,256]{0,1:T(8,128)S(1)} all-gather(f32[16,8]{0,1:T(8,128)S(1)} %copy-done.3), channel_id=1, replica_groups=mesh['gx'=4,'gy'=8] {'gx','gy'}, dimensions={1}, use_global_device_ids=true | all-gather | bytes 16896 | tf_op jit(solution)/shard_map/all_gather | solution.py:39
  122.5 0.1 copy.12
  122.6 0.1 constant_dynamic-slice_fusion
  122.7 0.7 copy.14
  123.4 0.0 copy-start.5
  123.4 0.0 copy-start.2
  123.4 0.0 copy-start.4
  123.4 5.6 %copy.13 = f32[256,4096]{0,1:T(8,128)} copy(f32[256,4096]{1,0:T(8,128)} %copy-done.1) | data formatting | bytes 8388608 | tf_op jit(solution)/shard_map/exp | solution.py:11
  129.0 0.0 copy-done.5
  129.0 2.8 %gather_fusion.1 = f32[64,256]{1,0:T(8,128)S(1)} fusion(f32[256,4096]{0,1:T(8,128)} %copy.13, s32[1024]{0:T(1024)S(1)} %pad_clamp_fusion), kind=kCustom, calls=%fused_computation.1 | custom fusion | bytes 131328 | tf_op jit(solution)/shard_map/jit(_take)/gather | solution.py:32
  131.9 0.3 fusion.6
  132.1 0.0 copy-done.2
  132.2 0.2 convolution_bitcast_fusion.1
  132.4 49.0 %psum.23 = f32[128,16]{0,1:T(8,128)S(1)} all-reduce(f32[128,16]{0,1:T(8,128)S(1)} %convolution_bitcast_fusion.1), channel_id=1, replica_groups=mesh['gx'=4,'gy'=8] {'gx','gy'}, use_global_device_ids=true, to_apply=%region_4.5 | all-reduce | flops 2048 | bytes 16384 | tf_op jit(solution)/shard_map/psum | solution.py:15
  181.3 0.0 copy-done.4
  181.3 0.8 fusion.9
  (4 shorter events, 0.0 us)
Async XLA Ops:
  0.6 40.5 %copy-start = (f32[16,4096]{1,0:T(8,128)S(1)}, f32[16,4096]{1,0:T(8,128)}, u32[]{:S(2)}) copy-start(f32[16,4096]{1,0:T(8,128)} %param.8) | copy-start | bytes 786436
  39.2 1.9 %copy-start.1 = (f32[256,4096]{1,0:T(8,128)}, f32[256,4096]{1,0:T(8,128)S(1)}, u32[]{:S(2)}) copy-start(f32[256,4096]{1,0:T(8,128)S(1)} %fusion.5) | copy-start | bytes 12582916
  41.1 49.4 %copy-start.3 = (f32[16,8]{0,1:T(8,128)S(1)}, f32[16,8]{0,1:T(8,128)}, u32[]{:S(2)}) copy-start(f32[16,8]{0,1:T(8,128)} %param.9) | copy-start | bytes 1540
  123.4 5.6 %copy-start.5 = (s32[64]{0:T(128)S(1)}, s32[64]{0:T(128)}, u32[]{:S(2)}) copy-start(s32[64]{0:T(128)} %param.11) | copy-start | bytes 772
  123.4 8.8 %copy-start.2 = (f32[64,128]{1,0:T(8,128)S(1)}, f32[64,128]{1,0:T(8,128)}, u32[]{:S(2)}) copy-start(f32[64,128]{1,0:T(8,128)} %param.12) | copy-start | bytes 98308
  123.4 58.0 %copy-start.4 = (f32[128]{0:T(128)S(1)}, f32[128]{0:T(128)}, u32[]{:S(2)}) copy-start(f32[128]{0:T(128)} %param.13) | copy-start | bytes 1540
where the time goes:
time: 183 us; the launch traced here: 182 us
  blocking collectives  156 us (85%)
  local copies, waits for them, and re-layouts  13.7 us (7%)
  matrix products  8.4 us (5%)
  other arithmetic  3.13 us (2%)
    psum x1, blocking collectives, combine_projection(): return lax.psum(partial_projection, ('gx', 'gy'))  49 us
    all_gather x1, blocking collectives, on_device(): targets_full = lax.all_gather(targets, ('gx', 'gy'), axis=1, tiled=True)  32.1 us
    all_gather x1, blocking collectives, on_device(): rows_in = lax.all_gather(batch_local, ('gx', 'gy'), axis=0, tiled=True)  29.1 us
    psum x1, blocking collectives, on_device(): inner_sum = lax.psum(partial_prediction, 'gy')  25.5 us
    psum x1, blocking collectives, on_device(): reduced = lax.psum(inner_sum, 'gx')  20.5 us
    exp x1, local copies, waits for them, and re-layouts, kernel_tile(): return jnp.exp(-jnp.sqrt(jnp.maximum(squared, 1.0)) / width)  5.64 us
    dot_general x1, matrix products, kernel_tile(): inner = jnp.dot(points, others.T, preferred_element_type=jnp.float32)  3.82 us

commit v1 on v0

--- a/solution.py
+++ b/solution.py
@@ -34,7 +34,7 @@
     gathered = jnp.concatenate([predicted, carried], axis=0)
     partial_prediction = gathered[:outputs]
     carried = gathered[outputs:]
-    inner_sum = lax.psum(partial_prediction, "gy")
+    inner_sum = jnp.sum(lax.all_gather(partial_prediction, "gy"), axis=0)
     reduced = lax.psum(inner_sum, "gx")
     targets_full = lax.all_gather(targets, ("gx", "gy"), axis=1, tiled=True)
     residual_full = reduced - targets_full

time: 183 us -> 169 us (0.923)
  blocking collectives: 156 us -> 142 us
    psum x1 -> x0, blocking collectives: 25.5 us -> none  [on_device(): inner_sum = lax.psum(partial_prediction, 'gy')]
    all_gather x0 -> x1, blocking collectives: none -> 13.6 us  [on_device(): inner_sum = jnp.sum(lax.all_gather(partial_prediction, 'gy'), axis=0)]
    all_gather x1, blocking collectives: 32.1 us -> 29.9 us  [on_device(): targets_full = lax.all_gather(targets, ('gx', 'gy'), axis=1, tiled=True)]
where the time goes in v1:
time: 169 us; the launch traced here: 168 us
  blocking collectives  142 us (84%)
  local copies, waits for them, and re-layouts  13.7 us (8%)
  matrix products  8.3 us (5%)
  other arithmetic  3.14 us (2%)
    psum x1, blocking collectives, combine_projection(): return lax.psum(partial_projection, ('gx', 'gy'))  48.8 us
    all_gather x1, blocking collectives, on_device(): targets_full = lax.all_gather(targets, ('gx', 'gy'), axis=1, tiled=True)  29.9 us
    all_gather x1, blocking collectives, on_device(): rows_in = lax.all_gather(batch_local, ('gx', 'gy'), axis=0, tiled=True)  29.1 us
    psum x1, blocking collectives, on_device(): reduced = lax.psum(inner_sum, 'gx')  20.4 us
    all_gather x1, blocking collectives, on_device(): inner_sum = jnp.sum(lax.all_gather(partial_prediction, 'gy'), axis=0)  13.6 us
    exp x1, local copies, waits for them, and re-layouts, kernel_tile(): return jnp.exp(-jnp.sqrt(jnp.maximum(squared, 1.0)) / width)  5.64 us
    dot_general x1, matrix products, kernel_tile(): inner = jnp.dot(points, others.T, preferred_element_type=jnp.float32)  3.82 us

profile of v1, /device:TPU:14, one launch (start us, length us, event | category | flops | bytes accessed | tf_op | source)
XLA Modules:
  0.0 167.7 jit_solution(16811128615719097566)
XLA Ops:
  0.6 0.0 copy-start
  0.7 0.7 compare_and_fusion.1
  1.4 2.4 %gather_fusion = bf16[8,256]{1,0:T(8,128)(2,1)S(1)} fusion(bf16[4096,256]{1,0:T(8,128)(2,1)} %param.7, s32[1024]{0:T(1024)S(1)} %pad_clamp_fusion.1), kind=kCustom, calls=%fused_computation | custom fusion | bytes 8224 | tf_op jit(solution)/shard_map/jit(_take)/gather | solution.py:24
  3.8 0.1 broadcast_select_fusion
  3.9 29.1 %all_gather.12 = bf16[256,256]{1,0:T(8,128)(2,1)S(1)} all-gather(bf16[8,256]{1,0:T(8,128)(2,1)S(1)} %broadcast_select_fusion), channel_id=1, replica_groups=mesh['gx'=4,'gy'=8] {'gx','gy'}, dimensions={0}, use_global_device_ids=true | all-gather | bytes 135168 | tf_op jit(solution)/shard_map/all_gather | solution.py:26
  33.0 2.2 %multiply_reduce_fusion = f32[4096]{0:T(1024)S(1)} fusion(bf16[4096,256]{1,0:T(8,128)(2,1)} %param.7), kind=kLoop, calls=%fused_computation.9 | loop fusion | flops 3141632 | bytes 2113536 | tf_op jit(solution)/shard_map/reduce_sum | solution.py:25
  35.2 0.1 multiply_reduce_fusion.1
  35.3 3.8 %fusion.5 = f32[256,4096]{1,0:T(8,128)S(1)} fusion(bf16[256,256]{1,0:T(8,128)(2,1)S(1)} %all_gather.12, bf16[4096,256]{1,0:T(8,128)(2,1)} %param.7, f32[4096]{0:T(1024)S(1)} %multiply_reduce_fusion, f32[256]{0:T(256)S(1)} %multiply_reduce_fusion.1), kind=kOutput, calls=%fused_computation.8 | convolution fusion | flops 543162368 | bytes 6439936 | tf_op jit(solution)/shard_map/dot_general | solution.py:9
  39.2 0.0 copy-start.1
  39.2 1.9 %copy-done.1 = f32[256,4096]{1,0:T(8,128)} copy-done((f32[256,4096]{1,0:T(8,128)}, f32[256,4096]{1,0:T(8,128)S(1)}, u32[]{:S(2)}) %copy-start.1) | copy-done | bytes 4194328
  41.1 0.0 copy-done
  41.1 0.0 copy-start.3
  41.1 3.3 %convolution_bitcast_fusion = f32[16,256]{1,0:T(8,128)S(1)} fusion(f32[256,4096]{1,0:T(8,128)S(1)} %fusion.5, f32[16,4096]{1,0:T(8,128)S(1)} %copy-done), kind=kOutput, calls=%fused_computation.10 | convolution fusion | flops 201326592 | bytes 4472832 | tf_op jit(solution)/shard_map/dot_general | solution.py:29
  44.4 13.6 %all-gather = f32[128,256]{1,0:T(8,128)S(1)} all-gather(f32[16,256]{1,0:T(8,128)S(1)} %convolution_bitcast_fusion), channel_id=2, replica_groups=mesh['gx'=4,'gy'=8] {'gy'}, dimensions={0}, use_global_device_ids=true | all-gather | bytes 147456 | tf_op jit(solution)/shard_map/all_gather | solution.py:37
  58.1 20.4 %psum.14 = f32[16,256]{1,0:T(8,128)S(1)} all-reduce(f32[16,256]{1,0:T(8,128)S(1)} %reduce_sum.29), channel_id=1, replica_groups=mesh['gx'=4,'gy'=8] {'gx'}, use_global_device_ids=true, to_apply=%region_3.4 | all-reduce | flops 4096 | bytes 32768 | tf_op jit(solution)/shard_map/psum | solution.py:38
  78.5 0.0 copy-done.3
  78.5 29.9 %all_gather.15 = f32[16,256]{0,1:T(8,128)S(1)} all-gather(f32[16,8]{0,1:T(8,128)S(1)} %copy-done.3), channel_id=1, replica_groups=mesh['gx'=4,'gy'=8] {'gx','gy'}, dimensions={1}, use_global_device_ids=true | all-gather | bytes 16896 | tf_op jit(solution)/shard_map/all_gather | solution.py:39
  108.3 0.1 copy.13
  108.4 0.1 constant_dynamic-slice_fusion
  108.5 0.7 copy.15
  109.2 0.0 copy-start.5
  109.2 0.0 copy-start.2
  109.2 0.0 copy-start.4
  109.2 5.6 %copy.14 = f32[256,4096]{0,1:T(8,128)} copy(f32[256,4096]{1,0:T(8,128)} %copy-done.1) | data formatting | bytes 8388608 | tf_op jit(solution)/shard_map/exp | solution.py:11
  114.8 0.0 copy-done.5
  114.8 2.8 %gather_fusion.1 = f32[64,256]{1,0:T(8,128)S(1)} fusion(f32[256,4096]{0,1:T(8,128)} %copy.14, s32[1024]{0:T(1024)S(1)} %pad_clamp_fusion), kind=kCustom, calls=%fused_computation.1 | custom fusion | bytes 131328 | tf_op jit(solution)/shard_map/jit(_take)/gather | solution.py:32
  117.7 0.2 fusion.6
  117.9 0.0 copy-done.2
  117.9 0.1 convolution_bitcast_fusion.1
  118.1 48.8 %psum.15 = f32[128,16]{0,1:T(8,128)S(1)} all-reduce(f32[128,16]{0,1:T(8,128)S(1)} %convolution_bitcast_fusion.1), channel_id=1, replica_groups=mesh['gx'=4,'gy'=8] {'gx','gy'}, use_global_device_ids=true, to_apply=%region_4.5 | all-reduce | flops 2048 | bytes 16384 | tf_op jit(solution)/shard_map/psum | solution.py:15
  166.9 0.0 copy-done.4
  166.9 0.8 fusion.9
  (5 shorter events, 0.0 us)
Async XLA Ops:
  0.6 40.5 %copy-start = (f32[16,4096]{1,0:T(8,128)S(1)}, f32[16,4096]{1,0:T(8,128)}, u32[]{:S(2)}) copy-start(f32[16,4096]{1,0:T(8,128)} %param.8) | copy-start | bytes 786436
  39.2 1.9 %copy-start.1 = (f32[256,4096]{1,0:T(8,128)}, f32[256,4096]{1,0:T(8,128)S(1)}, u32[]{:S(2)}) copy-start(f32[256,4096]{1,0:T(8,128)S(1)} %fusion.5) | copy-start | bytes 12582916
  41.1 37.4 %copy-start.3 = (f32[16,8]{0,1:T(8,128)S(1)}, f32[16,8]{0,1:T(8,128)}, u32[]{:S(2)}) copy-start(f32[16,8]{0,1:T(8,128)} %param.9) | copy-start | bytes 1540
  109.2 5.6 %copy-start.5 = (s32[64]{0:T(128)S(1)}, s32[64]{0:T(128)}, u32[]{:S(2)}) copy-start(s32[64]{0:T(128)} %param.11) | copy-start | bytes 772
  109.2 8.7 %copy-start.2 = (f32[64,128]{1,0:T(8,128)S(1)}, f32[64,128]{1,0:T(8,128)}, u32[]{:S(2)}) copy-start(f32[64,128]{1,0:T(8,128)} %param.12) | copy-start | bytes 98308
  109.2 57.7 %copy-start.4 = (f32[128]{0:T(128)S(1)}, f32[128]{0:T(128)}, u32[]{:S(2)}) copy-start(f32[128]{0:T(128)} %param.13) | copy-start | bytes 1540
